TPU v7x, 32 devices: a whole 2x2x4 slice. The times are simulated.
32 devices in a mesh: gx: 2 (over y), gy: 4 (over x, core), gz: 4 (over z).
Axes of the slice: x: 2, y: 2, z: 4, core: 2. Of those that a mesh axis runs over, the one named last changes fastest.
Arguments:
- tokens: bfloat16 [256, 8192], P('gx', 'gy'), may hold values from -6 to 6
- cotangent: bfloat16 [256, 8192], P('gx', 'gy'), may hold values from -6 to 6
- gate_weight: bfloat16 [8192, 28672], P('gy', ('gx', 'gz')), may hold values from -5.7452426 to 5.7452426
- up_weight: bfloat16 [8192, 28672], P('gy', ('gx', 'gz')), may hold values from -5.7452426 to 5.7452426
- down_weight: bfloat16 [28672, 8192], P(('gx', 'gz'), 'gy'), may hold values from -3.0709613 to 3.0709613
- gate_reduce: bfloat16 [8192, 32], P('gy'), may hold values from -0.0625 to 0.0625
- gate_expand: bfloat16 [32, 28672], P(None, ('gx', 'gz')), may hold values from -5 to 5
- gate_magnitude: float32 [28672], P(('gx', 'gz')), may hold values from 0.5 to 2
- up_reduce: bfloat16 [8192, 32], P('gy'), may hold values from -0.0625 to 0.0625
- up_expand: bfloat16 [32, 28672], P(None, ('gx', 'gz')), may hold values from -5 to 5
- up_magnitude: float32 [28672], P(('gx', 'gz')), may hold values from 0.5 to 2
- down_reduce: bfloat16 [28672, 32], P(('gx', 'gz')), may hold values from -0.03125 to 0.03125
- down_expand: bfloat16 [32, 8192], P(None, 'gy'), may hold values from -5 to 5
- down_magnitude: float32 [8192], P('gy'), may hold values from 0.5 to 2
Outputs:
- output: bfloat16 [256, 8192], P('gx', 'gy')
- grad_tokens: bfloat16 [256, 8192], P('gx', 'gy')
- grad_gate_reduce: float32 [8192, 32], P('gy')
- grad_gate_expand: float32 [32, 28672], P(None, ('gx', 'gz'))
- grad_gate_magnitude: float32 [28672], P(('gx', 'gz'))
- grad_up_reduce: float32 [8192, 32], P('gy')
- grad_up_expand: float32 [32, 28672], P(None, ('gx', 'gz'))
- grad_up_magnitude: float32 [28672], P(('gx', 'gz'))
- grad_down_reduce: float32 [28672, 32], P(('gx', 'gz'))
- grad_down_expand: float32 [32, 8192], P(None, 'gy')
- grad_down_magnitude: float32 [8192], P('gy')
All inputs are finite; a program needn't handle non-finite values.
Results may differ from a plain program's by a relative error of at most 0.012.
Values may be sent and summed in bfloat16 or wider, within the bound.
No kernel may reach another device: no remote copies, remote signals or barrier semaphores. Data moves between devices by JAX's collectives and lax.ppermute only.
A program may use at most 128 MiB of HBM per device.

v0:
```python
import jax
import jax.numpy as jnp
from jax import lax
from jax.sharding import PartitionSpec as P

EPSILON = 1e-06


def tile_square(weight, reduce_in, expand_out):
    merged = weight.astype(jnp.float32) + jnp.dot(
        reduce_in, expand_out, preferred_element_type=jnp.float32
    )
    return jnp.sum(merged * merged, axis=0)


def share_rows(values, count):
    return lax.dynamic_slice_in_dim(values, lax.axis_index("gz") * count, count, 0)


def contract_last(left, right):
    return lax.dot_general(
        left, right, (((1,), (1,)), ((), ())), preferred_element_type=jnp.float32
    )


def contract_first(left, right):
    return lax.dot_general(
        left, right, (((0,), (0,)), ((), ())), preferred_element_type=jnp.float32
    )


def on_device(
    tokens,
    cotangent,
    gate_weight,
    up_weight,
    down_weight,
    gate_reduce,
    gate_expand,
    gate_magnitude,
    up_reduce,
    up_expand,
    up_magnitude,
    down_reduce,
    down_expand,
    down_magnitude,
):
    share_count = tokens.shape[0] // lax.axis_size("gz")
    square_gate = tile_square(gate_weight, gate_reduce, gate_expand)
    square_up = tile_square(up_weight, up_reduce, up_expand)
    square_down = tile_square(down_weight, down_reduce, down_expand)
    norm_down = jnp.sqrt(lax.psum(square_down, ("gx", "gz")) + EPSILON)
    scale_down = down_magnitude / norm_down
    all_tokens = lax.all_gather(tokens, "gx", axis=0, tiled=True)
    part_gate = jnp.dot(all_tokens, gate_weight, preferred_element_type=jnp.float32)
    part_up = jnp.dot(all_tokens, up_weight, preferred_element_type=jnp.float32)
    low_gate_part = jnp.dot(all_tokens, gate_reduce, preferred_element_type=jnp.float32)
    low_up_part = jnp.dot(all_tokens, up_reduce, preferred_element_type=jnp.float32)
    gate_lin, up_lin, gate_lowsum, up_lowsum = (
        lax.psum_scatter(part_gate, "gy", scatter_dimension=0, tiled=True),
        lax.psum_scatter(part_up, "gy", scatter_dimension=0, tiled=True),
        lax.psum_scatter(low_gate_part, "gy", scatter_dimension=0, tiled=True),
        lax.psum_scatter(low_up_part, "gy", scatter_dimension=0, tiled=True),
    )
    summed_gate, summed_up = lax.psum((square_gate, square_up), "gy")
    norm_gate = jnp.sqrt(summed_gate + EPSILON)
    norm_up = jnp.sqrt(summed_up + EPSILON)
    scale_gate = gate_magnitude / norm_gate
    scale_up = up_magnitude / norm_up
    gate_low = gate_lowsum.astype(jnp.bfloat16)
    up_low = up_lowsum.astype(jnp.bfloat16)
    gate_lin = gate_lin + jnp.dot(gate_low, gate_expand, preferred_element_type=jnp.float32)
    up_lin = up_lin + jnp.dot(up_low, up_expand, preferred_element_type=jnp.float32)
    gate_pre = gate_lin * scale_gate[None, :]
    up_pre = up_lin * scale_up[None, :]
    sigmoid_gate = jax.nn.sigmoid(gate_pre)
    active = gate_pre * sigmoid_gate
    hidden = (active * up_pre).astype(jnp.bfloat16)
    all_hidden = lax.all_gather(hidden, "gy", axis=0, tiled=True)
    part_down = jnp.dot(all_hidden, down_weight, preferred_element_type=jnp.float32)
    low_down_part = jnp.dot(all_hidden, down_reduce, preferred_element_type=jnp.float32)
    down_lin, down_lowsum = (
        lax.psum_scatter(part_down, "gx", scatter_dimension=0, tiled=True),
        lax.psum_scatter(low_down_part, "gx", scatter_dimension=0, tiled=True),
    )
    down_lin, down_lowsum = lax.psum((down_lin, down_lowsum), "gz")
    down_low = down_lowsum.astype(jnp.bfloat16)
    down_lin = down_lin + jnp.dot(down_low, down_expand, preferred_element_type=jnp.float32)
    output = (down_lin * scale_down[None, :]).astype(jnp.bfloat16)
    down_lin = share_rows(down_lin, share_count)
    down_low = share_rows(down_low, share_count)
    cot_float = cotangent.astype(jnp.float32)
    down_delta = (cot_float * scale_down[None, :]).astype(jnp.bfloat16)
    cot_share = share_rows(cot_float, share_count)
    delta_share = share_rows(down_delta, share_count)
    grad_down_magnitude = jnp.sum(cot_share * down_lin, axis=0) / norm_down
    grad_down_expand = contract_first(down_low, delta_share)
    grad_down_magnitude, grad_down_expand = lax.psum(
        (grad_down_magnitude, grad_down_expand), ("gx", "gz")
    )
    all_delta = lax.all_gather(down_delta, "gx", axis=0, tiled=True)
    part_hidden_grad = contract_last(all_delta, down_weight)
    part_down_back = contract_last(all_delta, down_expand)
    hidden_gradsum, down_backsum = (
        lax.psum_scatter(part_hidden_grad, "gy", scatter_dimension=0, tiled=True),
        lax.psum_scatter(part_down_back, "gy", scatter_dimension=0, tiled=True),
    )
    down_back = down_backsum.astype(jnp.bfloat16)
    hidden_grad = (hidden_gradsum + contract_last(down_back, down_reduce)).astype(jnp.bfloat16)
    grad_down_reduce = contract_first(hidden, down_back)
    hgrad_float = hidden_grad.astype(jnp.float32)
    gate_grad = hgrad_float * up_pre * sigmoid_gate * (1.0 + gate_pre * (1.0 - sigmoid_gate))
    up_grad = hgrad_float * active
    gate_delta = (gate_grad * scale_gate[None, :]).astype(jnp.bfloat16)
    up_delta = (up_grad * scale_up[None, :]).astype(jnp.bfloat16)
    grad_gate_magnitude = jnp.sum(gate_grad * gate_lin, axis=0) / norm_gate
    grad_up_magnitude = jnp.sum(up_grad * up_lin, axis=0) / norm_up
    grad_gate_expand = contract_first(gate_low, gate_delta)
    grad_up_expand = contract_first(up_low, up_delta)
    grad_down_reduce, grad_gate_magnitude, grad_up_magnitude, grad_gate_expand, grad_up_expand = (
        lax.psum(
            (
                grad_down_reduce,
                grad_gate_magnitude,
                grad_up_magnitude,
                grad_gate_expand,
                grad_up_expand,
            ),
            "gy",
        )
    )
    all_gate_delta, all_up_delta = (
        lax.all_gather(gate_delta, "gy", axis=0, tiled=True),
        lax.all_gather(up_delta, "gy", axis=0, tiled=True),
    )
    part_input = contract_last(all_gate_delta, gate_weight) + contract_last(all_up_delta, up_weight)
    part_gate_back = contract_last(all_gate_delta, gate_expand)
    part_up_back = contract_last(all_up_delta, up_expand)
    input_sum, gate_backsum, up_backsum = (
        lax.psum_scatter(part_input, "gx", scatter_dimension=0, tiled=True),
        lax.psum_scatter(part_gate_back, "gx", scatter_dimension=0, tiled=True),
        lax.psum_scatter(part_up_back, "gx", scatter_dimension=0, tiled=True),
    )
    input_sum, gate_backsum, up_backsum = lax.psum((input_sum, gate_backsum, up_backsum), "gz")
    gate_back = gate_backsum.astype(jnp.bfloat16)
    up_back = up_backsum.astype(jnp.bfloat16)
    grad_tokens = (
        input_sum + contract_last(gate_back, gate_reduce) + contract_last(up_back, up_reduce)
    ).astype(jnp.bfloat16)
    gate_back = share_rows(gate_back, share_count)
    up_back = share_rows(up_back, share_count)
    token_share = share_rows(tokens, share_count)
    grad_gate_reduce = contract_first(token_share, gate_back)
    grad_up_reduce = contract_first(token_share, up_back)
    grad_gate_reduce, grad_up_reduce = lax.psum((grad_gate_reduce, grad_up_reduce), ("gx", "gz"))
    return (
        output,
        grad_tokens,
        grad_gate_reduce,
        grad_gate_expand,
        grad_gate_magnitude,
        grad_up_reduce,
        grad_up_expand,
        grad_up_magnitude,
        grad_down_reduce,
        grad_down_expand,
        grad_down_magnitude,
    )


def solution(mesh):
    return jax.shard_map(
        on_device,
        mesh=mesh,
        in_specs=(
            P("gx", "gy"),
            P("gx", "gy"),
            P("gy", ("gx", "gz")),
            P("gy", ("gx", "gz")),
            P(("gx", "gz"), "gy"),
            P("gy", None),
            P(None, ("gx", "gz")),
            P(("gx", "gz")),
            P("gy", None),
            P(None, ("gx", "gz")),
            P(("gx", "gz")),
            P(("gx", "gz"), None),
            P(None, "gy"),
            P("gy"),
        ),
        out_specs=(
            P("gx", "gy"),
            P("gx", "gy"),
            P("gy", None),
            P(None, ("gx", "gz")),
            P(("gx", "gz")),
            P("gy", None),
            P(None, ("gx", "gz")),
            P(("gx", "gz")),
            P(("gx", "gz"), None),
            P(None, "gy"),
            P("gy"),
        ),
        check_vma=False,
    )
```

profile of v0, /device:TPU:0, one launch (start us, length us, event | category | flops | bytes accessed | tf_op | source)
XLA Modules:
  0.0 689.7 jit_solution(911645773237748030)
XLA Ops:
  7.3 9.5 %multiply_reduce_fusion = f32[2048]{0:T(1024)S(1)} fusion(bf16[3584,2048]{1,0:T(8,128)(2,1)} %param.18, bf16[3584,32]{0,1:T(8,128)(2,1)} %param.25, bf16[32,2048]{1,0:T(8,128)(2,1)} %param.26), kind=kOutput, calls=%fused_computation | convolution fusion | flops 499120128 | bytes 15048704 | tf_op jit(solution)/shard_map/dot_general | solution.py:10
  16.8 23.7 %psum.123 = f32[2048]{0:T(1024)S(1)} all-reduce(f32[2048]{0:T(1024)S(1)} %multiply_reduce_fusion), channel_id=1, replica_groups=mesh['gx'=2,'gy'=4,'gz'=4] {'gx','gz'}, use_global_device_ids=true, to_apply=%region_13.0 | all-reduce | flops 2048 | bytes 16384 | tf_op jit(solution)/shard_map/psum | solution.py:52
  42.3 17.9 %all-gather.10.cloned.1.call-done = bf16[256,2048]{1,0:T(8,128)(2,1)} async-done(((bf16[128,2048]{1,0:T(8,128)(2,1)}), bf16[256,2048]{1,0:T(8,128)(2,1)}) %all-gather.10.cloned.1.call-update) | async-done | bytes 1048592 | tf_op jit(solution)/shard_map/all_gather | solution.py:101
  62.6 20.5 %all-gather.6.cloned.1.call-done = bf16[256,2048]{1,0:T(8,128)(2,1)} async-done(((bf16[128,2048]{1,0:T(8,128)(2,1)}), bf16[256,2048]{1,0:T(8,128)(2,1)}) %all-gather.6.cloned.1.call-update) | async-done | bytes 1048592 | tf_op jit(solution)/shard_map/all_gather | solution.py:54
  87.8 11.4 %fusion.37 = f32[256,3584]{1,0:T(8,128)} fusion(bf16[256,2048]{1,0:T(8,128)(2,1)} %all-gather.10.cloned.1.call-done, bf16[3584,2048]{1,0:T(8,128)(2,1)} %param.18), kind=kOutput, calls=%fused_computation.60 | convolution fusion | flops 3758096384 | bytes 19398656 | tf_op jit(solution)/shard_map/dot_general | solution.py:21
  99.3 9.1 %fusion.31 = f32[256,3584]{1,0:T(8,128)} fusion(bf16[256,2048]{1,0:T(8,128)(2,1)S(1)} %copy-done.1, bf16[2048,3584]{1,0:T(8,128)(2,1)} %param.16), kind=kOutput, calls=%fused_computation.54 | convolution fusion | flops 3758096384 | bytes 19398656 | tf_op jit(solution)/shard_map/dot_general | solution.py:55
  108.7 9.2 %fusion.33 = f32[256,3584]{1,0:T(8,128)} fusion(bf16[256,2048]{1,0:T(8,128)(2,1)S(1)} %copy-done.1, bf16[2048,3584]{1,0:T(8,128)(2,1)} %param.17), kind=kOutput, calls=%fused_computation.56 | convolution fusion | flops 3758096384 | bytes 19398656 | tf_op jit(solution)/shard_map/dot_general | solution.py:56
  117.9 7.5 %multiply_reduce_fusion.1 = f32[3584]{0:T(1024)S(1)} fusion(bf16[2048,3584]{1,0:T(8,128)(2,1)} %param.17, bf16[2048,32]{0,1:T(8,128)(2,1)S(1)} %copy-done.10, bf16[32,3584]{1,0:T(8,128)(2,1)S(1)} %copy-done), kind=kOutput, calls=%fused_computation.1 | convolution fusion | flops 499118592 | bytes 15054848 | tf_op jit(solution)/shard_map/dot_general | solution.py:10
  125.5 7.6 %multiply_reduce_fusion.2 = f32[3584]{0:T(1024)S(1)} fusion(bf16[2048,3584]{1,0:T(8,128)(2,1)} %param.16, bf16[2048,32]{0,1:T(8,128)(2,1)S(1)} %copy-done.9, bf16[32,3584]{1,0:T(8,128)(2,1)S(1)} %copy-done.7), kind=kOutput, calls=%fused_computation.2 | convolution fusion | flops 499118592 | bytes 15054848 | tf_op jit(solution)/shard_map/dot_general | solution.py:10
  133.1 10.9 %all-reduce.4 = (f32[3584]{0:T(1024)S(1)}, f32[3584]{0:T(1024)S(1)}) all-reduce(f32[3584]{0:T(1024)S(1)} %multiply_reduce_fusion.1, f32[3584]{0:T(1024)S(1)} %multiply_reduce_fusion.2), channel_id=1, replica_groups=mesh['gx'=2,'gy'=4,'gz'=4] {'gy'}, use_global_device_ids=true, to_apply=%region_7.0 | all-reduce | flops 7168 | bytes 57344 | tf_op jit(solution)/shard_map/psum | solution.py:65
  146.3 4.5 reduce-scatter.36.cloned.1.call-done
  151.6 42.8 %reduce-scatter.26.cloned.1.call-done = f32[64,3584]{1,0:T(8,128)} async-done(((f32[256,3584]{1,0:T(8,128)}), f32[64,3584]{1,0:T(8,128)}) %reduce-scatter.26.cloned.1.call-update) | async-done | bytes 917520 | tf_op jit(solution)/shard_map/reduce_scatter | solution.py:105
  195.9 42.3 %reduce-scatter.18.cloned.1.call-done = f32[64,3584]{1,0:T(8,128)} async-done(((f32[256,3584]{1,0:T(8,128)}), f32[64,3584]{1,0:T(8,128)}) %reduce-scatter.18.cloned.1.call-update) | async-done | bytes 917520 | tf_op jit(solution)/shard_map/reduce_scatter | solution.py:60
  239.7 42.3 %reduce-scatter.20.cloned.1.call-done = f32[64,3584]{1,0:T(8,128)} async-done(((f32[256,3584]{1,0:T(8,128)}), f32[64,3584]{1,0:T(8,128)}) %reduce-scatter.20.cloned.1.call-update) | async-done | bytes 917520 | tf_op jit(solution)/shard_map/reduce_scatter | solution.py:61
  282.1 3.5 multiply_reduce_fusion.3
  288.0 19.6 %all-gather.12.cloned.1.call-done = bf16[256,3584]{1,0:T(8,128)(2,1)} async-done(((bf16[64,3584]{1,0:T(8,128)(2,1)}), bf16[256,3584]{1,0:T(8,128)(2,1)}) %all-gather.12.cloned.1.call-update) | async-done | bytes 1835024 | tf_op jit(solution)/shard_map/all_gather | solution.py:133
  307.7 11.0 %fusion.39 = f32[256,2048]{1,0:T(8,128)} fusion(bf16[256,3584]{1,0:T(8,128)(2,1)} %all-gather.12.cloned.1.call-done, bf16[2048,3584]{1,0:T(8,128)(2,1)} %param.16), kind=kOutput, calls=%fused_computation.62 | convolution fusion | flops 3758096384 | bytes 18612224 | tf_op jit(solution)/shard_map/dot_general | solution.py:21
  318.7 12.1 %all-gather.14.cloned.1.call-done = bf16[256,3584]{1,0:T(8,128)(2,1)} async-done(((bf16[64,3584]{1,0:T(8,128)(2,1)}), bf16[256,3584]{1,0:T(8,128)(2,1)}) %all-gather.14.cloned.1.call-update) | async-done | bytes 1835024 | tf_op jit(solution)/shard_map/all_gather | solution.py:134
  330.8 11.6 %convolution_add_fusion.3 = f32[256,2048]{1,0:T(8,128)} fusion(f32[256,2048]{1,0:T(8,128)} %fusion.39, bf16[256,3584]{1,0:T(8,128)(2,1)} %all-gather.14.cloned.1.call-done, bf16[2048,3584]{1,0:T(8,128)(2,1)} %param.17), kind=kOutput, calls=%fused_computation.8 | convolution fusion | flops 3758620672 | bytes 20709376 | tf_op jit(solution)/shard_map/dot_general | solution.py:21
  342.5 11.6 %all-gather.8.cloned.1.call-done = bf16[256,3584]{1,0:T(8,128)(2,1)} async-done(((bf16[64,3584]{1,0:T(8,128)(2,1)}), bf16[256,3584]{1,0:T(8,128)(2,1)}) %all-gather.8.cloned.1.call-update) | async-done | bytes 1835024 | tf_op jit(solution)/shard_map/all_gather | solution.py:79
  354.1 11.0 %fusion.35 = f32[256,2048]{1,0:T(8,128)} fusion(bf16[256,3584]{1,0:T(8,128)(2,1)} %all-gather.8.cloned.1.call-done, bf16[3584,2048]{1,0:T(8,128)(2,1)} %param.18), kind=kOutput, calls=%fused_computation.58 | convolution fusion | flops 3758096384 | bytes 18612224 | tf_op jit(solution)/shard_map/dot_general | solution.py:80
  370.9 2.8 fusion.41
  373.7 14.4 %reduce-scatter.28.cloned.1.call-done = f32[128,2048]{1,0:T(8,128)} async-done(((f32[256,2048]{1,0:T(8,128)}), f32[128,2048]{1,0:T(8,128)}) %reduce-scatter.28.cloned.1.call-update) | async-done | bytes 1048592 | tf_op jit(solution)/shard_map/reduce_scatter | solution.py:140
  388.1 34.2 %reduce-scatter.22.cloned.1.call-done = f32[128,2048]{1,0:T(8,128)} async-done(((f32[256,2048]{1,0:T(8,128)}), f32[128,2048]{1,0:T(8,128)}) %reduce-scatter.22.cloned.1.call-update) | async-done | bytes 1048592 | tf_op jit(solution)/shard_map/reduce_scatter | solution.py:83
  427.0 11.5 %all-reduce.3 = (f32[3584]{0:T(1024)}, f32[3584]{0:T(1024)}) all-reduce(f32[3584]{0:T(1024)S(1)} %get-tuple-element.33, f32[3584]{0:T(1024)S(1)} %get-tuple-element.34), channel_id=1, replica_groups=mesh['gx'=2,'gy'=4,'gz'=4] {'gy'}, use_global_device_ids=true, to_apply=%region_25.0 | all-reduce | flops 7168 | bytes 57344 | tf_op jit(solution)/shard_map/psum | solution.py:121
  438.5 9.1 %reduce-scatter.24.cloned.1.call-done = f32[128,32]{0,1:T(8,128)} async-done(((f32[256,32]{0,1:T(8,128)}), f32[128,32]{0,1:T(8,128)}) %reduce-scatter.24.cloned.1.call-update) | async-done | bytes 16400 | tf_op jit(solution)/shard_map/reduce_scatter | solution.py:84
  447.5 12.6 %reduce-scatter.32.cloned.1.call-done = f32[128,32]{0,1:T(8,128)} async-done(((f32[256,32]{0,1:T(8,128)}), f32[128,32]{0,1:T(8,128)}) %reduce-scatter.32.cloned.1.call-update) | async-done | bytes 16400 | tf_op jit(solution)/shard_map/reduce_scatter | solution.py:142
  460.1 21.1 %all-reduce.1 = (bf16[128,32]{0,1:T(8,128)(2,1)S(1)}, bf16[128,32]{0,1:T(8,128)(2,1)S(1)}, bf16[128,32]{0,1:T(8,128)(2,1)S(1)}) all-reduce(f32[128,32]{0,1:T(8,128)} %reduce-scatter.24.cloned.1.call-done, f32[128,32]{0,1:T(8,128)} %reduce-scatter.30.cloned.1.call-done, ...), channel_id=1, replica_groups=mesh['gx'=2,'gy'=4,'gz'=4] {'gz'}, use_global_device_ids=true, to_apply=%region_11.0 | all-reduce | flops 12288 | bytes 73728 | tf_op jit(solution)/shard_map/psum | solution.py:86
  485.0 64.4 %all-reduce.12.cloned.1.call-done = (f32[128,2048]{1,0:T(8,128)}, f32[128,2048]{1,0:T(8,128)}) async-done(((f32[128,2048]{1,0:T(8,128)}, f32[128,2048]{1,0:T(8,128)}), (f32[128,2048]{1,0:T(8,128)}, f32[128,2048]{1,0:T(8,128)})) %all-reduce.12.cloned.1.call-update) | async-done | bytes 2097168 | tf_op jit(solution)/shard_map/psum | solution.py:86
  551.8 20.5 %psum.135 = f32[2048]{0:T(1024)} all-reduce(f32[2048]{0:T(1024)S(1)} %fusion.17), channel_id=1, replica_groups=mesh['gx'=2,'gy'=4,'gz'=4] {'gx','gz'}, use_global_device_ids=true, to_apply=%region_33.0 | all-reduce | flops 2048 | bytes 16384 | tf_op jit(solution)/shard_map/psum | solution.py:98
  574.9 17.2 %all-reduce.14.cloned.1.call-done = (f32[32,3584]{1,0:T(8,128)}, f32[32,3584]{1,0:T(8,128)}, f32[3584,32]{0,1:T(8,128)}) async-done(((f32[32,3584]{1,0:T(8,128)}, f32[32,3584]{1,0:T(8,128)}, f32[3584,32]{0,1:T(8,128)}), (f32[32,3584]{1,0:T(8,128)}, f32[32,3584]{1,0:T(8,128)}, f32[3584,32]{0,1:T(8,128)})) %all-reduce.14.cloned.1.call-update) | async-done | bytes 1376272 | tf_op jit(solution)/shard_map/psum | solution.py:121
  592.1 80.6 %all-reduce.10.cloned.1.call-done = (f32[2048,32]{0,1:T(8,128)}, f32[2048,32]{0,1:T(8,128)}, f32[32,2048]{1,0:T(8,128)}) async-done(((f32[2048,32]{0,1:T(8,128)}, f32[2048,32]{0,1:T(8,128)}, f32[32,2048]{1,0:T(8,128)}), (f32[2048,32]{0,1:T(8,128)}, f32[2048,32]{0,1:T(8,128)}, f32[32,2048]{1,0:T(8,128)})) %all-reduce.10.cloned.1.call-update) | async-done | bytes 786448 | tf_op jit(solution)/shard_map/psum | solution.py:155
  (109 shorter events, 47.3 us)
Async XLA Ops:
  7.2 110.7 %copy-start = (bf16[32,3584]{1,0:T(8,128)(2,1)S(1)}, bf16[32,3584]{1,0:T(8,128)(2,1)}, u32[]{:S(2)}) copy-start(bf16[32,3584]{1,0:T(8,128)(2,1)} %param.23) | copy-start | bytes 688132
  7.2 33.3 %copy-start.16 = (f32[2048]{0:T(1024)S(1)}, f32[2048]{0:T(1024)}, u32[]{:S(2)}) copy-start(f32[2048]{0:T(1024)} %param.27) | copy-start | bytes 24580
  7.2 33.4 %copy-start.3 = (bf16[128,2048]{1,0:T(8,128)(2,1)S(1)}, bf16[128,2048]{1,0:T(8,128)(2,1)}, u32[]{:S(2)}) copy-start(bf16[128,2048]{1,0:T(8,128)(2,1)} %param.15) | copy-start | bytes 1572868
  7.2 53.0 %copy-start.11 = (bf16[32,2048]{1,0:T(8,128)(2,1)S(1)}, bf16[32,2048]{1,0:T(8,128)(2,1)}, u32[]{:S(2)}) copy-start(bf16[32,2048]{1,0:T(8,128)(2,1)} %param.26) | copy-start | bytes 393220
  7.2 75.8 %copy-start.9 = (bf16[2048,32]{0,1:T(8,128)(2,1)S(1)}, bf16[2048,32]{0,1:T(8,128)(2,1)}, u32[]{:S(2)}) copy-start(bf16[2048,32]{0,1:T(8,128)(2,1)} %param.19) | copy-start | bytes 393220
  7.2 78.2 %copy-start.10 = (bf16[2048,32]{0,1:T(8,128)(2,1)S(1)}, bf16[2048,32]{0,1:T(8,128)(2,1)}, u32[]{:S(2)}) copy-start(bf16[2048,32]{0,1:T(8,128)(2,1)} %param.22) | copy-start | bytes 393220
  7.2 52.9 %all-gather.10.cloned.1.call-start = ((), (), s32[]{:S(2)}) async-start(), calls=%async_computation.17 | async-start | bytes 1572864 | tf_op jit(solution)/shard_map/all_gather | solution.py:101
  41.5 41.5 %all-gather.6.cloned.1.call-start = ((), (), s32[]{:S(2)}) async-start(), calls=%async_computation.11 | async-start | bytes 1572864 | tf_op jit(solution)/shard_map/all_gather | solution.py:54
  42.2 102.3 %reduce-scatter.38.cloned.1.call-start = ((), (), s32[]{:S(2)}) async-start(), calls=%async_computation.26 | async-start | bytes 163840
  62.5 82.9 %reduce-scatter.34.cloned.1.call-start = ((), (), s32[]{:S(2)}) async-start(), calls=%async_computation.24 | async-start | bytes 163840
  85.4 65.4 %reduce-scatter.36.cloned.1.call-start = ((), (), s32[]{:S(2)}) async-start(), calls=%async_computation.25 | async-start | bytes 163840
  87.8 106.7 %reduce-scatter.26.cloned.1.call-start = ((), (), s32[]{:S(2)}) async-start(), calls=%async_computation.18 | async-start | bytes 4587520 | tf_op jit(solution)/shard_map/reduce_scatter | solution.py:105
  99.2 139.0 %reduce-scatter.18.cloned.1.call-start = ((), (), s32[]{:S(2)}) async-start(), calls=%async_computation.12 | async-start | bytes 4587520 | tf_op jit(solution)/shard_map/reduce_scatter | solution.py:60
  108.4 173.6 %reduce-scatter.20.cloned.1.call-start = ((), (), s32[]{:S(2)}) async-start(), calls=%async_computation.13 | async-start | bytes 4587520 | tf_op jit(solution)/shard_map/reduce_scatter | solution.py:61
  117.9 189.8 %all-gather.12.cloned.1.call-start = ((), (), s32[]{:S(2)}) async-start(), calls=%async_computation.19 | async-start | bytes 2293760 | tf_op jit(solution)/shard_map/all_gather | solution.py:133
  125.5 18.6 %copy-start.15 = (f32[3584]{0:T(1024)S(1)}, f32[3584]{0:T(1024)}, u32[]{:S(2)}) copy-start(f32[3584]{0:T(1024)} %param.24) | copy-start | bytes 43012
  125.5 68.9 %copy-start.8 = (bf16[3584,32]{0,1:T(8,128)(2,1)S(1)}, bf16[3584,32]{0,1:T(8,128)(2,1)}, u32[]{:S(2)}) copy-start(bf16[3584,32]{0,1:T(8,128)(2,1)} %param.25) | copy-start | bytes 688132
  151.6 167.1 %copy-start.13 = (bf16[64,32]{0,1:T(8,128)(2,1)}, bf16[64,32]{0,1:T(8,128)(2,1)S(1)}, u32[]{:S(2)}) copy-start(bf16[64,32]{0,1:T(8,128)(2,1)S(1)} %copy.28) | copy-start | bytes 12292
  286.5 44.4 %all-gather.14.cloned.1.call-start = ((), (), s32[]{:S(2)}) async-start(), calls=%async_computation.20 | async-start | bytes 2293760 | tf_op jit(solution)/shard_map/all_gather | solution.py:134
  287.0 67.0 %all-gather.8.cloned.1.call-start = ((), (), s32[]{:S(2)}) async-start(), calls=%async_computation.14 | async-start | bytes 2293760 | tf_op jit(solution)/shard_map/all_gather | solution.py:79
  287.8 100.3 %reduce-scatter.28.cloned.1.call-start = ((), (), s32[]{:S(2)}) async-start(), calls=%async_computation.21 | async-start | bytes 3145728 | tf_op jit(solution)/shard_map/reduce_scatter | solution.py:140
  342.4 80.0 %copy-start.2 = (bf16[64,3584]{1,0:T(8,128)(2,1)S(1)}, bf16[64,3584]{1,0:T(8,128)(2,1)}, u32[]{:S(2)}) copy-start(bf16[64,3584]{1,0:T(8,128)(2,1)} %multiply_convert_fusion.3) | copy-start | bytes 1376260
  342.4 80.9 %copy-start.5 = (bf16[64,3584]{1,0:T(8,128)(2,1)S(1)}, bf16[64,3584]{1,0:T(8,128)(2,1)}, u32[]{:S(2)}) copy-start(bf16[64,3584]{1,0:T(8,128)(2,1)} %get-tuple-element.30) | copy-start | bytes 1376260
  342.4 81.9 %copy-start.4 = (bf16[64,3584]{1,0:T(8,128)(2,1)S(1)}, bf16[64,3584]{1,0:T(8,128)(2,1)}, u32[]{:S(2)}) copy-start(bf16[64,3584]{1,0:T(8,128)(2,1)} %get-tuple-element.29) | copy-start | bytes 1376260
  342.5 79.8 %reduce-scatter.22.cloned.1.call-start = ((), (), s32[]{:S(2)}) async-start(), calls=%async_computation.15 | async-start | bytes 3145728 | tf_op jit(solution)/shard_map/reduce_scatter | solution.py:83
  365.1 118.0 %copy-start.6 = (bf16[128,2048]{1,0:T(8,128)(2,1)S(1)}, bf16[128,2048]{1,0:T(8,128)(2,1)}, u32[]{:S(2)}) copy-start(bf16[128,2048]{1,0:T(8,128)(2,1)} %param.14) | copy-start | bytes 1572868
  365.1 73.3 %reduce-scatter.30.cloned.1.call-start = ((), (), s32[]{:S(2)}) async-start(), calls=%async_computation.22 | async-start | bytes 49152 | tf_op jit(solution)/shard_map/reduce_scatter | solution.py:141
  368.0 79.5 %reduce-scatter.24.cloned.1.call-start = ((), (), s32[]{:S(2)}) async-start(), calls=%async_computation.16 | async-start | bytes 49152 | tf_op jit(solution)/shard_map/reduce_scatter | solution.py:84
  370.8 89.3 %reduce-scatter.32.cloned.1.call-start = ((), (), s32[]{:S(2)}) async-start(), calls=%async_computation.23 | async-start | bytes 49152 | tf_op jit(solution)/shard_map/reduce_scatter | solution.py:142
  373.7 175.7 %all-reduce.12.cloned.1.call-start = ((), (), s32[]{:S(2)}) async-start(), calls=%async_computation.28 | async-start | bytes 4194304 | tf_op jit(solution)/shard_map/psum | solution.py:86
  422.3 169.8 %all-reduce.14.cloned.1.call-start = ((), (), s32[]{:S(2)}) async-start(), calls=%async_computation.29 | async-start | bytes 2752512 | tf_op jit(solution)/shard_map/psum | solution.py:121
  426.0 246.7 %all-reduce.10.cloned.1.call-start = ((), (), s32[]{:S(2)}) async-start(), calls=%async_computation.27 | async-start | bytes 1572864 | tf_op jit(solution)/shard_map/psum | solution.py:155
  (4 other events, 38.3 us)
Sparse Core Ops, SparseCore 0:
  41.6 18.5 all-gather.9
  61.7 21.2 all-gather.5
  86.0 19.6 reduce-scatter.37
  108.5 19.6 reduce-scatter.33
  131.1 19.6 reduce-scatter.35
  153.1 41.2 reduce-scatter.25
  197.0 41.2 reduce-scatter.17
  240.8 41.2 reduce-scatter.19
  286.6 21.0 all-gather.11
  309.7 21.0 all-gather.13
  332.9 21.0 all-gather.7
  356.2 31.8 reduce-scatter.27
  390.4 31.8 reduce-scatter.21
  424.9 9.9 reduce-scatter.29
  437.5 9.9 reduce-scatter.23
  450.1 9.9 reduce-scatter.31
  462.4 86.9 all-reduce.11
  552.9 39.1 all-reduce.13
  597.0 75.6 all-reduce.9
where the time goes:
time: 691 us; the launch traced here: 690 us
  waiting for transfers between devices  448 us (65%)
  matrix products  122 us (18%)
  blocking collectives  87.7 us (13%)
  between operations  14.4 us (2%)
  local copies, waits for them, and re-layouts  13.6 us (2%)
    psum x1, waiting for transfers between devices, on_device(): lax.psum((grad_gate_reduce, grad_up_reduce), ('gx', 'gz'))  80.6 us
    psum x1, waiting for transfers between devices, on_device(): down_lin, down_lowsum = lax.psum((down_lin, down_lowsum), 'gz')  64.4 us
    dot_general x8, matrix products, contract_last(): lax.dot_general(left, right, (((1,), (1,)), ((), ())), preferred_element_...  43.7 us
    reduce_scatter x1, waiting for transfers between devices, on_device(): lax.psum_scatter(part_hidden_grad, 'gy', scatter_dimension=0, tiled=True)  42.8 us
    reduce_scatter x1, waiting for transfers between devices, on_device(): lax.psum_scatter(part_gate, 'gy', scatter_dimension=0, tiled=True)  42.3 us
    reduce_scatter x1, waiting for transfers between devices, on_device(): lax.psum_scatter(part_up, 'gy', scatter_dimension=0, tiled=True)  42.3 us
    reduce_scatter x1, waiting for transfers between devices, on_device(): lax.psum_scatter(part_down, 'gx', scatter_dimension=0, tiled=True)  34.2 us
    dot_general x3, matrix products, tile_square(): jnp.dot(reduce_in, expand_out, preferred_element_type=jnp.float32)  24.6 us
  transfers between devices with their start and end apart: 19, of which 16 were waited for; matrix products, arithmetic and copies ran while one was open for 16% of the time, Pallas kernels for 0%

commit v1 on v0

v1 whole, which is shorter than its diff:
```python
import jax
import jax.numpy as jnp
from jax import lax
from jax.sharding import PartitionSpec as P

EPSILON = 1e-06


def tile_square(weight, reduce_in, expand_out):
    merged = weight.astype(jnp.float32) + jnp.dot(
        reduce_in, expand_out, preferred_element_type=jnp.float32
    )
    return jnp.sum(merged * merged, axis=0)


def swap(values, axis, bit):
    count = lax.axis_size(axis)
    return lax.ppermute(values, axis, [(i, i ^ bit) for i in range(count)])


def all_sum(values, *axes):
    for axis in axes:
        bit = 1
        while bit < lax.axis_size(axis):
            values = values + swap(values, axis, bit)
            bit *= 2
    return values


def own_rows(values, axis):
    rows = values.shape[0] // lax.axis_size(axis)
    return lax.dynamic_slice_in_dim(values, lax.axis_index(axis) * rows, rows, 0)


def flip(values, axis):
    count = lax.axis_size(axis)
    rows = values.shape[0] // count
    index = lax.axis_index(axis)
    return jnp.concatenate(
        [
            lax.dynamic_slice_in_dim(values, jnp.bitwise_xor(index, p) * rows, rows, 0)
            for p in range(count)
        ],
        axis=0,
    )


def scatter_sum(values, axis):
    count = lax.axis_size(axis)
    rows, columns = values.shape
    block = rows // count
    values = values.astype(jnp.bfloat16).reshape(count, block, columns)
    bit = 1
    while bit < count:
        pairs = values.reshape(values.shape[0] // 2, 2, block, columns)
        got = swap(pairs[:, 1], axis, bit)
        values = pairs[:, 0].astype(jnp.float32) + got.astype(jnp.float32)
        bit *= 2
        if bit < count:
            values = values.astype(jnp.bfloat16)
    return values.reshape(block, columns)


def gather(values, axis):
    count = lax.axis_size(axis)
    block, columns = values.shape
    values = values.reshape(1, block, columns)
    bit = count // 2
    while bit >= 1:
        got = swap(values, axis, bit)
        values = jnp.stack([values, got], axis=1).reshape(-1, block, columns)
        bit //= 2
    return flip(values.reshape(count * block, columns), axis)


def contract_last(left, right):
    return lax.dot_general(
        left, right, (((1,), (1,)), ((), ())), preferred_element_type=jnp.float32
    )


def contract_first(left, right):
    return lax.dot_general(
        left, right, (((0,), (0,)), ((), ())), preferred_element_type=jnp.float32
    )


def on_device(
    tokens,
    cotangent,
    gate_weight,
    up_weight,
    down_weight,
    gate_reduce,
    gate_expand,
    gate_magnitude,
    up_reduce,
    up_expand,
    up_magnitude,
    down_reduce,
    down_expand,
    down_magnitude,
):
    bf16 = jnp.bfloat16
    f32 = jnp.float32
    rank = gate_reduce.shape[1]
    all_tokens = gather(tokens, "gx")
    all_cot = gather(cotangent, "gx")
    square_down = tile_square(down_weight, down_reduce, down_expand)
    norm_down = jnp.sqrt(all_sum(square_down, "gx", "gz") + EPSILON)
    scale_down = down_magnitude / norm_down

    turned = flip(all_tokens, "gy")
    part_gate = jnp.dot(turned, gate_weight, preferred_element_type=f32)
    gate_sum = scatter_sum(part_gate, "gy")
    part_up = jnp.dot(turned, up_weight, preferred_element_type=f32)
    up_sum = scatter_sum(part_up, "gy")
    both_reduce = jnp.concatenate([gate_reduce, up_reduce], axis=1)
    low_sum = all_sum(jnp.dot(all_tokens, both_reduce, preferred_element_type=f32), "gy").astype(bf16)
    gate_low, up_low = low_sum[:, :rank], low_sum[:, rank:]

    square_gate = tile_square(gate_weight, gate_reduce, gate_expand)
    square_up = tile_square(up_weight, up_reduce, up_expand)
    squares = all_sum(jnp.stack([square_gate, square_up]), "gy")
    norm_gate = jnp.sqrt(squares[0] + EPSILON)
    norm_up = jnp.sqrt(squares[1] + EPSILON)
    scale_gate = gate_magnitude / norm_gate
    scale_up = up_magnitude / norm_up

    all_delta = (all_cot.astype(f32) * scale_down[None, :]).astype(bf16)
    part_hidden_grad = contract_last(flip(all_delta, "gy"), down_weight)
    hidden_gradsum = scatter_sum(part_hidden_grad, "gy")
    down_back = all_sum(contract_last(all_delta, down_expand), "gy").astype(bf16)

    low_own = own_rows(low_sum, "gy")
    gate_lin = gate_sum + jnp.dot(low_own[:, :rank], gate_expand, preferred_element_type=f32)
    up_lin = up_sum + jnp.dot(low_own[:, rank:], up_expand, preferred_element_type=f32)
    gate_pre = gate_lin * scale_gate[None, :]
    up_pre = up_lin * scale_up[None, :]
    sigmoid_gate = jax.nn.sigmoid(gate_pre)
    active = gate_pre * sigmoid_gate
    hidden = (active * up_pre).astype(bf16)
    all_hidden = gather(hidden, "gy")

    hidden_grad = (
        hidden_gradsum + contract_last(own_rows(down_back, "gy"), down_reduce)
    ).astype(bf16)
    hgrad_float = hidden_grad.astype(f32)
    gate_grad = hgrad_float * up_pre * sigmoid_gate * (1.0 + gate_pre * (1.0 - sigmoid_gate))
    up_grad = hgrad_float * active
    gate_delta = (gate_grad * scale_gate[None, :]).astype(bf16)
    up_delta = (up_grad * scale_up[None, :]).astype(bf16)
    all_gate_delta = gather(gate_delta, "gy")
    all_up_delta = gather(up_delta, "gy")
    magnitudes = all_sum(
        jnp.stack([jnp.sum(gate_grad * gate_lin, axis=0), jnp.sum(up_grad * up_lin, axis=0)]),
        "gy",
    )
    grad_gate_magnitude = magnitudes[0] / norm_gate
    grad_up_magnitude = magnitudes[1] / norm_up

    part_down = jnp.dot(all_hidden, down_weight, preferred_element_type=f32).astype(bf16)
    down_rows = scatter_sum(flip(part_down, "gx"), "gx").astype(bf16)
    down_rows = scatter_sum(flip(down_rows, "gz"), "gz")
    down_low = all_sum(
        jnp.dot(all_hidden, down_reduce, preferred_element_type=f32), "gx", "gz"
    ).astype(bf16)
    low_rows = own_rows(own_rows(down_low, "gx"), "gz")
    down_lin = down_rows + jnp.dot(low_rows, down_expand, preferred_element_type=f32)
    output = gather((down_lin * scale_down[None, :]).astype(bf16), "gz")
    cot_rows = own_rows(cotangent, "gz").astype(f32)
    grad_down_magnitude = (
        all_sum(jnp.sum(cot_rows * down_lin, axis=0), "gx", "gz") / norm_down
    )
    grad_down_expand = contract_first(down_low, all_delta)
    grad_down_reduce = contract_first(all_hidden, down_back)

    part_input = contract_last(all_gate_delta, gate_weight) + contract_last(all_up_delta, up_weight)
    input_rows = scatter_sum(flip(part_input.astype(bf16), "gx"), "gx").astype(bf16)
    input_rows = scatter_sum(flip(input_rows, "gz"), "gz")
    backs = all_sum(
        jnp.concatenate(
            [
                contract_last(all_gate_delta, gate_expand),
                contract_last(all_up_delta, up_expand),
            ],
            axis=1,
        ),
        "gx",
        "gz",
    ).astype(bf16)
    gate_back, up_back = backs[:, :rank], backs[:, rank:]
    back_rows = own_rows(own_rows(backs, "gx"), "gz")
    grad_tokens = gather(
        (input_rows + contract_last(back_rows, both_reduce)).astype(bf16), "gz"
    )
    grad_gate_expand = contract_first(gate_low, all_gate_delta)
    grad_up_expand = contract_first(up_low, all_up_delta)
    grad_gate_reduce = contract_first(all_tokens, gate_back)
    grad_up_reduce = contract_first(all_tokens, up_back)
    return (
        output,
        grad_tokens,
        grad_gate_reduce,
        grad_gate_expand,
        grad_gate_magnitude,
        grad_up_reduce,
        grad_up_expand,
        grad_up_magnitude,
        grad_down_reduce,
        grad_down_expand,
        grad_down_magnitude,
    )


def solution(mesh):
    return jax.shard_map(
        on_device,
        mesh=mesh,
        in_specs=(
            P("gx", "gy"),
            P("gx", "gy"),
            P("gy", ("gx", "gz")),
            P("gy", ("gx", "gz")),
            P(("gx", "gz"), "gy"),
            P("gy", None),
            P(None, ("gx", "gz")),
            P(("gx", "gz")),
            P("gy", None),
            P(None, ("gx", "gz")),
            P(("gx", "gz")),
            P(("gx", "gz"), None),
            P(None, "gy"),
            P("gy"),
        ),
        out_specs=(
            P("gx", "gy"),
            P("gx", "gy"),
            P("gy", None),
            P(None, ("gx", "gz")),
            P(("gx", "gz")),
            P("gy", None),
            P(None, ("gx", "gz")),
            P(("gx", "gz")),
            P(("gx", "gz"), None),
            P(None, "gy"),
            P("gy"),
        ),
        check_vma=False,
    )
```

time: 691 us -> 261 us (0.38)
  waiting for transfers between devices: 448 us -> 86.2 us
  blocking collectives: 87.7 us -> 0 us
  starting transfers between devices: 1.18 us -> 53.5 us
  matrix products: 122 us -> 91.2 us
  between operations: 14.4 us -> 2.31 us
  other arithmetic: 2.68 us -> 12.6 us
    reduce_scatter x8 -> x0, waiting for transfers between devices: 198 us -> none  [the longest x1 42.8 us: on_device(): lax.psum_scatter(part_hidden_grad, 'gy', scatter_dimension=0, tiled=True)]
    psum x3 -> x0, waiting for transfers between devices: 162 us -> none  [the longest x1 80.6 us: on_device(): lax.psum((grad_gate_reduce, grad_up_reduce), ('gx', 'gz'))]
    psum x5 -> x0, blocking collectives: 87.7 us -> none  [the longest x1 23.7 us: on_device(): norm_down = jnp.sqrt(lax.psum(square_down, ('gx', 'gz')) + EPSILON)]
    ppermute x0 -> x44, waiting for transfers between devices: none -> 86.2 us  [swap(): return lax.ppermute(values, axis, [(i, i ^ bit) for i in range(count)])]
    all_gather x5 -> x0, waiting for transfers between devices: 81.7 us -> none  [the longest x1 20.5 us: on_device(): all_tokens = lax.all_gather(tokens, 'gx', axis=0, tiled=True)]
    ppermute x0 -> x44, starting transfers between devices: none -> 53.5 us  [swap(): return lax.ppermute(values, axis, [(i, i ^ bit) for i in range(count)])]
    dot_general x7 -> x8, matrix products: 39.4 us -> 23.8 us  [the longest x1 9.48 us: on_device(): part_gate = jnp.dot(turned, gate_weight, preferred_element_type=f32)]
    unnamed x43 -> x97, local copies, waits for them, and re-layouts: 13.6 us -> 5.2 us
  transfers between devices with their start and end apart: 19 -> 44, of which waited for: 16 -> 23; matrix products, arithmetic and copies ran while one was open for 16% -> 29% of each run, Pallas kernels for 0% -> 0%
where the time goes in v1:
time: 261 us; the launch traced here: 257 us
  matrix products  91.2 us (35%)
  waiting for transfers between devices  86.2 us (33%)
  starting transfers between devices  53.5 us (20%)
  other arithmetic  12.6 us (5%)
  local copies, waits for them, and re-layouts  11.5 us (4%)
    ppermute x44, waiting for transfers between devices, swap(): return lax.ppermute(values, axis, [(i, i ^ bit) for i in range(count)])  86.2 us
    ppermute x44, starting transfers between devices, swap(): return lax.ppermute(values, axis, [(i, i ^ bit) for i in range(count)])  53.5 us
    dot_general x8, matrix products, contract_last(): lax.dot_general(left, right, (((1,), (1,)), ((), ())), preferred_element_...  36.1 us
    dot_general x3, matrix products, tile_square(): jnp.dot(reduce_in, expand_out, preferred_element_type=jnp.float32)  24.7 us
    dot_general x1, matrix products, on_device(): part_gate = jnp.dot(turned, gate_weight, preferred_element_type=f32)  9.48 us
    dot_general x6, matrix products, contract_first(): lax.dot_general(left, right, (((0,), (0,)), ((), ())), preferred_element_...  6.68 us
    dot_general x1, matrix products, on_device(): part_up = jnp.dot(turned, up_weight, preferred_element_type=f32)  5.42 us
  transfers between devices with their start and end apart: 44, of which 23 were waited for; matrix products, arithmetic and copies ran while one was open for 29% of the time, Pallas kernels for 0%

profile of v1, /device:TPU:0, one launch (start us, length us, event | category | flops | bytes accessed | tf_op | source)
XLA Modules:
  0.0 257.4 jit_solution(5631862284419141783)
XLA Ops:
  0.7 3.1 %collective-permute-start = (bf16[1,128,2048]{2,1,0:T(8,128)(2,1)}, bf16[1,128,2048]{2,1,0:T(8,128)(2,1)S(1)}, u32[]{:S(2)}, u32[]{:S(2)}) collective-permute-start(bf16[1,128,2048]{2,1,0:T(8,128)(2,1)} %bitcast.276), channel_id=1, source_target_pairs={{0,16},{16,0},{1,17},{17,1},{2,18},{18,2},{3,19},{19,3},{4,20},{20... | collective-permute-start | bytes 1572872 | tf_op jit(solution)/shard_map/ppermute | solution.py:18
  3.8 9.4 %multiply_reduce_fusion = f32[2048]{0:T(1024)S(1)} fusion(bf16[3584,2048]{1,0:T(8,128)(2,1)} %param.18, bf16[3584,32]{0,1:T(8,128)(2,1)} %param.25, bf16[32,2048]{1,0:T(8,128)(2,1)} %param.26), kind=kOutput, calls=%fused_computation | convolution fusion | flops 499120128 | bytes 15048704 | tf_op jit(solution)/shard_map/dot_general | solution.py:10
  13.3 2.0 collective-permute-start.17
  15.3 7.7 %multiply_reduce_fusion.2 = f32[3584]{0:T(1024)S(1)} fusion(bf16[2048,3584]{1,0:T(8,128)(2,1)} %param.16, bf16[2048,32]{0,1:T(8,128)(2,1)S(1)} %copy-done.27, bf16[32,3584]{1,0:T(8,128)(2,1)S(1)} %copy-done), kind=kOutput, calls=%fused_computation.2 | convolution fusion | flops 499118592 | bytes 15054848 | tf_op jit(solution)/shard_map/dot_general | solution.py:10
  23.0 7.6 %multiply_reduce_fusion.1 = f32[3584]{0:T(1024)S(1)} fusion(bf16[2048,3584]{1,0:T(8,128)(2,1)} %param.17, bf16[2048,32]{0,1:T(8,128)(2,1)S(1)} %copy-done.28, bf16[32,3584]{1,0:T(8,128)(2,1)S(1)} %copy-done.21), kind=kOutput, calls=%fused_computation.1 | convolution fusion | flops 499118592 | bytes 15054848 | tf_op jit(solution)/shard_map/dot_general | solution.py:10
  32.5 2.0 collective-permute-done.18
  34.5 2.6 %collective-permute-start.19 = (f32[2048]{0:T(1024)S(1)}, f32[2048]{0:T(1024)S(1)}, u32[]{:S(2)}, u32[]{:S(2)}) collective-permute-start(f32[2048]{0:T(1024)S(1)} %add.252), channel_id=1, source_target_pairs={{0,2},{1,3},{2,0},{3,1},{4,6},{5,7},{6,4},{7,5},{8,10},{9,11},{10,... | collective-permute-start | bytes 24584 | tf_op jit(solution)/shard_map/ppermute | solution.py:18
  46.7 9.5 %convolution_convert_fusion.2 = bf16[256,3584]{1,0:T(8,128)(2,1)S(1)} fusion(bf16[2048,3584]{1,0:T(8,128)(2,1)} %param.16, bf16[64,2048]{1,0:T(8,128)(2,1)S(1)} %get-tuple-element.45, bf16[64,2048]{1,0:T(8,128)(2,1)S(1)} %get-tuple-element.44, bf16[64,2048]{1,0:T(8,128)(2,1)S(1)} %get-tuple-element.43, bf16[64,2048]{1,0:T(8,128)(2,1)S(1)} %get-tuple-element.42), kind=kOutput, calls=%fused_computation.5 | convolution fusion | flops 3763208192 | bytes 17563648 | tf_op jit(solution)/shard_map/dot_general | solution.py:114
  56.3 5.4 %convolution_convert_fusion.1 = bf16[256,3584]{1,0:T(8,128)(2,1)} fusion(bf16[2048,3584]{1,0:T(8,128)(2,1)S(1)} %bitcast.298, bf16[64,2048]{1,0:T(8,128)(2,1)S(1)} %get-tuple-element.45, bf16[64,2048]{1,0:T(8,128)(2,1)S(1)} %get-tuple-element.44, bf16[64,2048]{1,0:T(8,128)(2,1)S(1)} %get-tuple-element.43, bf16[64,2048]{1,0:T(8,128)(2,1)S(1)} %get-tuple-element.42), kind=kOutput, calls=%fused_computation.4 | convolution fusion | flops 3763208192 | bytes 17563648 | tf_op jit(solution)/shard_map/dot_general | solution.py:116
  61.9 10.8 %convolution_convert_fusion = bf16[256,3584]{1,0:T(8,128)(2,1)} fusion(bf16[3584,2048]{1,0:T(8,128)(2,1)} %param.18, bf16[64,2048]{1,0:T(8,128)(2,1)} %get-tuple-element.35, bf16[64,2048]{1,0:T(8,128)(2,1)} %get-tuple-element.36, bf16[64,2048]{1,0:T(8,128)(2,1)} %get-tuple-element.37, bf16[64,2048]{1,0:T(8,128)(2,1)} %get-tuple-element.34), kind=kOutput, calls=%fused_computation.3 | convolution fusion | flops 3763208192 | bytes 17563648 | tf_op jit(solution)/shard_map/dot_general | solution.py:77
  80.8 2.3 collective-permute-done.4
  87.9 8.9 %collective-permute-done.24 = bf16[1,64,3584]{2,1,0:T(8,128)(2,1)S(1)} collective-permute-done((bf16[1,64,3584]{2,1,0:T(8,128)(2,1)S(1)}, bf16[1,64,3584]{2,1,0:T(8,128)(2,1)S(1)}, u32[]{:S(2)}, u32[]{:S(2)}) %collective-permute-start.24) | collective-permute-done | bytes 458784 | tf_op jit(solution)/shard_map/ppermute | solution.py:18
  97.2 9.4 %collective-permute-done.8 = bf16[1,64,3584]{2,1,0:T(8,128)(2,1)S(1)} collective-permute-done((bf16[1,64,3584]{2,1,0:T(8,128)(2,1)S(1)}, bf16[1,64,3584]{2,1,0:T(8,128)(2,1)S(1)}, u32[]{:S(2)}, u32[]{:S(2)}) %collective-permute-start.8) | collective-permute-done | bytes 458784 | tf_op jit(solution)/shard_map/ppermute | solution.py:18
  107.0 8.0 %collective-permute-done.2 = bf16[1,64,3584]{2,1,0:T(8,128)(2,1)S(1)} collective-permute-done((bf16[1,64,3584]{2,1,0:T(8,128)(2,1)S(1)}, bf16[1,64,3584]{2,1,0:T(8,128)(2,1)S(1)}, u32[]{:S(2)}, u32[]{:S(2)}) %collective-permute-start.2) | collective-permute-done | bytes 458784 | tf_op jit(solution)/shard_map/ppermute | solution.py:18
  115.1 2.1 multiply_reduce_fusion.4
  121.7 19.7 %collective-permute-done.40 = f32[2,3584]{1,0:T(2,128)S(1)} collective-permute-done((f32[2,3584]{1,0:T(2,128)S(1)}, f32[2,3584]{1,0:T(2,128)S(1)}, u32[]{:S(2)}, u32[]{:S(2)}) %collective-permute-start.40) | collective-permute-done | bytes 28704 | tf_op jit(solution)/shard_map/ppermute | solution.py:18
  143.7 7.0 %collective-permute-done.27 = bf16[1,64,3584]{2,1,0:T(8,128)(2,1)S(1)} collective-permute-done((bf16[1,64,3584]{2,1,0:T(8,128)(2,1)S(1)}, bf16[1,64,3584]{2,1,0:T(8,128)(2,1)S(1)}, u32[]{:S(2)}, u32[]{:S(2)}) %collective-permute-start.27) | collective-permute-done | bytes 458784 | tf_op jit(solution)/shard_map/ppermute | solution.py:18
  159.4 4.2 %convolution_convert_fusion.3 = bf16[256,2048]{1,0:T(8,128)(2,1)S(1)} fusion(bf16[3584,2048]{1,0:T(8,128)(2,1)S(1)} %bitcast.296, bf16[64,3584]{1,0:T(8,128)(2,1)S(1)} %get-tuple-element.28, bf16[64,3584]{1,0:T(8,128)(2,1)S(1)} %get-tuple-element.29, bf16[64,3584]{1,0:T(8,128)(2,1)S(1)} %get-tuple-element.30, bf16[64,3584]{1,0:T(8,128)(2,1)S(1)} %get-tuple-element.27), kind=kOutput, calls=%fused_computation.8 | convolution fusion | flops 3765960704 | bytes 17563648 | tf_op jit(solution)/shard_map/dot_general | solution.py:162
  166.1 11.1 %fusion.88 = f32[256,2048]{1,0:T(8,128)} fusion(bf16[2048,3584]{1,0:T(8,128)(2,1)} %param.16, bf16[64,3584]{1,0:T(8,128)(2,1)} %copy-done.16, bf16[64,3584]{1,0:T(8,128)(2,1)} %copy-done.17, bf16[64,3584]{1,0:T(8,128)(2,1)} %copy-done.18, bf16[64,3584]{1,0:T(8,128)(2,1)} %copy-done.15), kind=kOutput, calls=%fused_computation.228 | convolution fusion | flops 3765436416 | bytes 18612224 | tf_op jit(solution)/shard_map/dot_general | solution.py:77
  181.3 11.3 %fusion = bf16[256,2048]{1,0:T(8,128)(2,1)} fusion(f32[256,2048]{1,0:T(8,128)} %fusion.88, bf16[2048,3584]{1,0:T(8,128)(2,1)} %param.17, bf16[64,3584]{1,0:T(8,128)(2,1)} %copy-done.12, bf16[64,3584]{1,0:T(8,128)(2,1)} %copy-done.13, bf16[64,3584]{1,0:T(8,128)(2,1)} %copy-done.14, bf16[64,3584]{1,0:T(8,128)(2,1)} %copy-done.11), kind=kOutput, calls=%fused_computation.7 | convolution fusion | flops 3766484992 | bytes 19660800 | tf_op jit(solution)/shard_map/dot_general | solution.py:77
  201.6 2.0 collective-permute-done.16
  204.3 1.8 collective-permute-start.36
  207.1 2.4 collective-permute-done.36
  214.3 6.5 %collective-permute-done.12 = bf16[2,32,2048]{2,1,0:T(8,128)(2,1)S(1)} collective-permute-done((bf16[2,32,2048]{2,1,0:T(8,128)(2,1)S(1)}, bf16[2,32,2048]{2,1,0:T(8,128)(2,1)S(1)}, u32[]{:S(2)}, u32[]{:S(2)}) %collective-permute-start.12) | collective-permute-done | bytes 262176 | tf_op jit(solution)/shard_map/ppermute | solution.py:18
  220.9 2.1 collective-permute-start.13
  224.4 2.7 %collective-permute-start.33 = (bf16[1,32,2048]{2,1,0:T(8,128)(2,1)S(1)}, bf16[1,32,2048]{2,1,0:T(8,128)(2,1)S(1)}, u32[]{:S(2)}, u32[]{:S(2)}) collective-permute-start(bf16[1,32,2048]{2,1,0:T(8,128)(2,1)S(1)} %slice_bitcast_fusion.20), channel_id=1, source_target_pairs={{0,2},{1,3},{2,0},{3,1},{4,6},{5,7},{6,4},{7,5},{8,10},{9,11},{10,... | collective-permute-start | bytes 393224 | tf_op jit(solution)/shard_map/ppermute | solution.py:18
  229.8 6.6 %collective-permute-start.41 = (f32[2048]{0:T(1024)S(1)}, f32[2048]{0:T(1024)S(1)}, u32[]{:S(2)}, u32[]{:S(2)}) collective-permute-start(f32[2048]{0:T(1024)S(1)} %get-tuple-element.56), channel_id=1, source_target_pairs={{0,16},{16,0},{1,17},{17,1},{2,18},{18,2},{3,19},{19,3},{4,20},{20... | collective-permute-start | bytes 24584 | tf_op jit(solution)/shard_map/ppermute | solution.py:18
  238.0 3.2 %collective-permute-start.42 = (f32[2048]{0:T(1024)S(1)}, f32[2048]{0:T(1024)S(1)}, u32[]{:S(2)}, u32[]{:S(2)}) collective-permute-start(f32[2048]{0:T(1024)S(1)} %add.272), channel_id=1, source_target_pairs={{0,1},{1,0},{2,3},{3,2},{4,5},{5,4},{6,7},{7,6},{8,9},{9,8},{10,11... | collective-permute-start | bytes 24584 | tf_op jit(solution)/shard_map/ppermute | solution.py:18
  243.1 2.6 %collective-permute-start.43 = (f32[2048]{0:T(1024)S(1)}, f32[2048]{0:T(1024)S(1)}, u32[]{:S(2)}, u32[]{:S(2)}) collective-permute-start(f32[2048]{0:T(1024)S(1)} %add.273), channel_id=1, source_target_pairs={{0,2},{1,3},{2,0},{3,1},{4,6},{5,7},{6,4},{7,5},{8,10},{9,11},{10,... | collective-permute-start | bytes 24584 | tf_op jit(solution)/shard_map/ppermute | solution.py:18
  246.2 2.1 collective-permute-done.37
  249.1 3.1 %collective-permute-done.21 = bf16[2,32,2048]{2,1,0:T(8,128)(2,1)S(1)} collective-permute-done((bf16[2,32,2048]{2,1,0:T(8,128)(2,1)S(1)}, bf16[2,32,2048]{2,1,0:T(8,128)(2,1)S(1)}, u32[]{:S(2)}, u32[]{:S(2)}) %collective-permute-start.21) | collective-permute-done | bytes 262176 | tf_op jit(solution)/shard_map/ppermute | solution.py:18
  252.3 2.7 %collective-permute-done.38 = bf16[2,32,2048]{2,1,0:T(8,128)(2,1)S(1)} collective-permute-done((bf16[2,32,2048]{2,1,0:T(8,128)(2,1)S(1)}, bf16[2,32,2048]{2,1,0:T(8,128)(2,1)S(1)}, u32[]{:S(2)}, u32[]{:S(2)}) %collective-permute-start.38) | collective-permute-done | bytes 262176 | tf_op jit(solution)/shard_map/ppermute | solution.py:18
  (270 shorter events, 73.1 us)
Async XLA Ops:
  0.7 41.9 %collective-permute-start = (bf16[1,128,2048]{2,1,0:T(8,128)(2,1)}, bf16[1,128,2048]{2,1,0:T(8,128)(2,1)S(1)}, u32[]{:S(2)}, u32[]{:S(2)}) collective-permute-start(bf16[1,128,2048]{2,1,0:T(8,128)(2,1)} %bitcast.276), channel_id=1, source_target_pairs={{0,16},{16,0},{1,17},{17,1},{2,18},{18,2},{3,19},{19,3},{4,20},{20... | collective-permute-start | bytes 1572872 | tf_op jit(solution)/shard_map/ppermute | solution.py:18
  3.7 38.9 %collective-permute-start.22 = (bf16[1,128,2048]{2,1,0:T(8,128)(2,1)}, bf16[1,128,2048]{2,1,0:T(8,128)(2,1)S(1)}, u32[]{:S(2)}, u32[]{:S(2)}) collective-permute-start(bf16[1,128,2048]{2,1,0:T(8,128)(2,1)} %bitcast.274), channel_id=1, source_target_pairs={{0,16},{16,0},{1,17},{17,1},{2,18},{18,2},{3,19},{19,3},{4,20},{20... | collective-permute-start | bytes 1572872 | tf_op jit(solution)/shard_map/ppermute | solution.py:18
  13.3 17.5 %collective-permute-start.17 = (f32[2048]{0:T(1024)S(1)}, f32[2048]{0:T(1024)S(1)}, u32[]{:S(2)}, u32[]{:S(2)}) collective-permute-start(f32[2048]{0:T(1024)S(1)} %multiply_reduce_fusion), channel_id=1, source_target_pairs={{0,16},{16,0},{1,17},{17,1},{2,18},{18,2},{3,19},{19,3},{4,20},{20... | collective-permute-start | bytes 24584 | tf_op jit(solution)/shard_map/ppermute | solution.py:18
  30.7 6.4 %collective-permute-start.5 = (f32[2,3584]{1,0:T(2,128)S(1)}, f32[2,3584]{1,0:T(2,128)S(1)}, u32[]{:S(2)}, u32[]{:S(2)}) collective-permute-start(f32[2,3584]{1,0:T(2,128)S(1)} %pad_maximum_fusion.29), channel_id=1, source_target_pairs={{0,4},{4,0},{8,12},{12,8},{1,5},{5,1},{9,13},{13,9},{2,6},{6,2},{1... | collective-permute-start | bytes 86024 | tf_op jit(solution)/shard_map/ppermute | solution.py:18
  61.8 24.0 %collective-permute-start.1 = (bf16[2,64,3584]{2,1,0:T(8,128)(2,1)S(1)}, bf16[2,64,3584]{2,1,0:T(8,128)(2,1)}, u32[]{:S(2)}, u32[]{:S(2)}) collective-permute-start(bf16[2,64,3584]{2,1,0:T(8,128)(2,1)S(1)} %slice_bitcast_fusion.4), channel_id=1, source_target_pairs={{0,4},{4,0},{8,12},{12,8},{1,5},{5,1},{9,13},{13,9},{2,6},{6,2},{1... | collective-permute-start | bytes 2752520 | tf_op jit(solution)/shard_map/ppermute | solution.py:18
  74.1 9.0 %collective-permute-start.23 = (bf16[2,64,3584]{2,1,0:T(8,128)(2,1)S(1)}, bf16[2,64,3584]{2,1,0:T(8,128)(2,1)S(1)}, u32[]{:S(2)}, u32[]{:S(2)}) collective-permute-start(bf16[2,64,3584]{2,1,0:T(8,128)(2,1)S(1)} %slice_bitcast_fusion), channel_id=1, source_target_pairs={{0,4},{4,0},{8,12},{12,8},{1,5},{5,1},{9,13},{13,9},{2,6},{6,2},{1... | collective-permute-start | bytes 2752520 | tf_op jit(solution)/shard_map/ppermute | solution.py:18
  78.4 5.6 %collective-permute-start.7 = (bf16[2,64,3584]{2,1,0:T(8,128)(2,1)S(1)}, bf16[2,64,3584]{2,1,0:T(8,128)(2,1)S(1)}, u32[]{:S(2)}, u32[]{:S(2)}) collective-permute-start(bf16[2,64,3584]{2,1,0:T(8,128)(2,1)S(1)} %slice_bitcast_fusion.2), channel_id=1, source_target_pairs={{0,4},{4,0},{8,12},{12,8},{1,5},{5,1},{9,13},{13,9},{2,6},{6,2},{1... | collective-permute-start | bytes 2752520 | tf_op jit(solution)/shard_map/ppermute | solution.py:18
  83.4 13.5 %collective-permute-start.24 = (bf16[1,64,3584]{2,1,0:T(8,128)(2,1)S(1)}, bf16[1,64,3584]{2,1,0:T(8,128)(2,1)S(1)}, u32[]{:S(2)}, u32[]{:S(2)}) collective-permute-start(bf16[1,64,3584]{2,1,0:T(8,128)(2,1)S(1)} %slice_bitcast_fusion.10), channel_id=1, source_target_pairs={{0,8},{4,12},{8,0},{12,4},{1,9},{5,13},{9,1},{13,5},{2,10},{6,14},... | collective-permute-start | bytes 1376264 | tf_op jit(solution)/shard_map/ppermute | solution.py:18
  84.3 22.3 %collective-permute-start.8 = (bf16[1,64,3584]{2,1,0:T(8,128)(2,1)S(1)}, bf16[1,64,3584]{2,1,0:T(8,128)(2,1)S(1)}, u32[]{:S(2)}, u32[]{:S(2)}) collective-permute-start(bf16[1,64,3584]{2,1,0:T(8,128)(2,1)S(1)} %slice_bitcast_fusion.12), channel_id=1, source_target_pairs={{0,8},{4,12},{8,0},{12,4},{1,9},{5,13},{9,1},{13,5},{2,10},{6,14},... | collective-permute-start | bytes 1376264 | tf_op jit(solution)/shard_map/ppermute | solution.py:18
  87.3 27.8 %collective-permute-start.2 = (bf16[1,64,3584]{2,1,0:T(8,128)(2,1)S(1)}, bf16[1,64,3584]{2,1,0:T(8,128)(2,1)S(1)}, u32[]{:S(2)}, u32[]{:S(2)}) collective-permute-start(bf16[1,64,3584]{2,1,0:T(8,128)(2,1)S(1)} %slice_bitcast_fusion.14), channel_id=1, source_target_pairs={{0,8},{4,12},{8,0},{12,4},{1,9},{5,13},{9,1},{13,5},{2,10},{6,14},... | collective-permute-start | bytes 1376264 | tf_op jit(solution)/shard_map/ppermute | solution.py:18
  117.3 25.5 %collective-permute-start.9 = (bf16[1,64,3584]{2,1,0:T(8,128)(2,1)}, bf16[1,64,3584]{2,1,0:T(8,128)(2,1)S(1)}, u32[]{:S(2)}, u32[]{:S(2)}) collective-permute-start(bf16[1,64,3584]{2,1,0:T(8,128)(2,1)} %bitcast.286), channel_id=1, source_target_pairs={{0,8},{4,12},{8,0},{12,4},{1,9},{5,13},{9,1},{13,5},{2,10},{6,14},... | collective-permute-start | bytes 1376264 | tf_op jit(solution)/shard_map/ppermute | solution.py:18
  118.1 25.0 %collective-permute-start.29 = (bf16[1,64,3584]{2,1,0:T(8,128)(2,1)}, bf16[1,64,3584]{2,1,0:T(8,128)(2,1)S(1)}, u32[]{:S(2)}, u32[]{:S(2)}) collective-permute-start(bf16[1,64,3584]{2,1,0:T(8,128)(2,1)} %bitcast.284), channel_id=1, source_target_pairs={{0,8},{4,12},{8,0},{12,4},{1,9},{5,13},{9,1},{13,5},{2,10},{6,14},... | collective-permute-start | bytes 1376264 | tf_op jit(solution)/shard_map/ppermute | solution.py:18
  119.5 22.0 %collective-permute-start.40 = (f32[2,3584]{1,0:T(2,128)S(1)}, f32[2,3584]{1,0:T(2,128)S(1)}, u32[]{:S(2)}, u32[]{:S(2)}) collective-permute-start(f32[2,3584]{1,0:T(2,128)S(1)} %fusion.84), channel_id=1, source_target_pairs={{0,8},{4,12},{8,0},{12,4},{1,9},{5,13},{9,1},{13,5},{2,10},{6,14},... | collective-permute-start | bytes 86024 | tf_op jit(solution)/shard_map/ppermute | solution.py:18
  120.3 30.4 %collective-permute-start.27 = (bf16[1,64,3584]{2,1,0:T(8,128)(2,1)S(1)}, bf16[1,64,3584]{2,1,0:T(8,128)(2,1)S(1)}, u32[]{:S(2)}, u32[]{:S(2)}) collective-permute-start(bf16[1,64,3584]{2,1,0:T(8,128)(2,1)S(1)} %get-tuple-element.49), channel_id=1, source_target_pairs={{0,8},{4,12},{8,0},{12,4},{1,9},{5,13},{9,1},{13,5},{2,10},{6,14},... | collective-permute-start | bytes 1376264 | tf_op jit(solution)/shard_map/ppermute | solution.py:18
  142.9 8.0 %collective-permute-start.10 = (bf16[2,64,3584]{2,1,0:T(8,128)(2,1)S(1)}, bf16[2,64,3584]{2,1,0:T(8,128)(2,1)S(1)}, u32[]{:S(2)}, u32[]{:S(2)}) collective-permute-start(bf16[2,64,3584]{2,1,0:T(8,128)(2,1)S(1)} %get-tuple-element.55), channel_id=1, source_target_pairs={{0,4},{4,0},{8,12},{12,8},{1,5},{5,1},{9,13},{13,9},{2,6},{6,2},{1... | collective-permute-start | bytes 2752520 | tf_op jit(solution)/shard_map/ppermute | solution.py:18
  143.2 20.5 %collective-permute-start.30 = (bf16[2,64,3584]{2,1,0:T(8,128)(2,1)S(1)}, bf16[2,64,3584]{2,1,0:T(8,128)(2,1)S(1)}, u32[]{:S(2)}, u32[]{:S(2)}) collective-permute-start(bf16[2,64,3584]{2,1,0:T(8,128)(2,1)S(1)} %get-tuple-element.51), channel_id=1, source_target_pairs={{0,4},{4,0},{8,12},{12,8},{1,5},{5,1},{9,13},{13,9},{2,6},{6,2},{1... | collective-permute-start | bytes 2752520 | tf_op jit(solution)/shard_map/ppermute | solution.py:18
  177.2 16.9 %collective-permute-start.14 = (f32[256,32]{0,1:T(8,128)S(1)}, f32[256,32]{0,1:T(8,128)}, u32[]{:S(2)}, u32[]{:S(2)}) collective-permute-start(f32[256,32]{0,1:T(8,128)S(1)} %fusion.90), channel_id=1, source_target_pairs={{0,16},{16,0},{1,17},{17,1},{2,18},{18,2},{3,19},{19,3},{4,20},{20... | collective-permute-start | bytes 98312 | tf_op jit(solution)/shard_map/ppermute | solution.py:18
  178.7 31.9 %collective-permute-start.11 = (bf16[1,128,2048]{2,1,0:T(8,128)(2,1)}, bf16[1,128,2048]{2,1,0:T(8,128)(2,1)}, u32[]{:S(2)}, u32[]{:S(2)}) collective-permute-start(bf16[1,128,2048]{2,1,0:T(8,128)(2,1)} %slice_bitcast_fusion.8), channel_id=1, source_target_pairs={{0,16},{16,0},{1,17},{17,1},{2,18},{18,2},{3,19},{19,3},{4,20},{20... | collective-permute-start | bytes 1572872 | tf_op jit(solution)/shard_map/ppermute | solution.py:18
  180.8 19.1 %collective-permute-start.34 = (f32[256,64]{0,1:T(8,128)}, f32[256,64]{0,1:T(8,128)S(1)}, u32[]{:S(2)}, u32[]{:S(2)}) collective-permute-start(f32[256,64]{0,1:T(8,128)} %pad_maximum_fusion.28), channel_id=1, source_target_pairs={{0,16},{16,0},{1,17},{17,1},{2,18},{18,2},{3,19},{19,3},{4,20},{20... | collective-permute-start | bytes 196616 | tf_op jit(solution)/shard_map/ppermute | solution.py:18
  196.5 17.0 %collective-permute-start.31 = (bf16[1,128,2048]{2,1,0:T(8,128)(2,1)S(1)}, bf16[1,128,2048]{2,1,0:T(8,128)(2,1)S(1)}, u32[]{:S(2)}, u32[]{:S(2)}) collective-permute-start(bf16[1,128,2048]{2,1,0:T(8,128)(2,1)S(1)} %slice_bitcast_fusion.6), channel_id=1, source_target_pairs={{0,16},{16,0},{1,17},{17,1},{2,18},{18,2},{3,19},{19,3},{4,20},{20... | collective-permute-start | bytes 1572872 | tf_op jit(solution)/shard_map/ppermute | solution.py:18
  204.3 5.2 %collective-permute-start.36 = (f32[256,64]{0,1:T(8,128)S(1)}, f32[256,64]{0,1:T(8,128)S(1)}, u32[]{:S(2)}, u32[]{:S(2)}) collective-permute-start(f32[256,64]{0,1:T(8,128)S(1)} %add.267), channel_id=1, source_target_pairs={{0,2},{1,3},{2,0},{3,1},{4,6},{5,7},{6,4},{7,5},{8,10},{9,11},{10,... | collective-permute-start | bytes 196616 | tf_op jit(solution)/shard_map/ppermute | solution.py:18
  211.8 9.0 %collective-permute-start.12 = (bf16[2,32,2048]{2,1,0:T(8,128)(2,1)S(1)}, bf16[2,32,2048]{2,1,0:T(8,128)(2,1)S(1)}, u32[]{:S(2)}, u32[]{:S(2)}) collective-permute-start(bf16[2,32,2048]{2,1,0:T(8,128)(2,1)S(1)} %slice_bitcast_fusion.18), channel_id=1, source_target_pairs={{0,1},{1,0},{2,3},{3,2},{4,5},{5,4},{6,7},{7,6},{8,9},{9,8},{10,11... | collective-permute-start | bytes 786440 | tf_op jit(solution)/shard_map/ppermute | solution.py:18
  213.8 10.6 %collective-permute-start.32 = (bf16[2,32,2048]{2,1,0:T(8,128)(2,1)S(1)}, bf16[2,32,2048]{2,1,0:T(8,128)(2,1)S(1)}, u32[]{:S(2)}, u32[]{:S(2)}) collective-permute-start(bf16[2,32,2048]{2,1,0:T(8,128)(2,1)S(1)} %slice_bitcast_fusion.16), channel_id=1, source_target_pairs={{0,1},{1,0},{2,3},{3,2},{4,5},{5,4},{6,7},{7,6},{8,9},{9,8},{10,11... | collective-permute-start | bytes 786440 | tf_op jit(solution)/shard_map/ppermute | solution.py:18
  220.9 7.6 %collective-permute-start.13 = (bf16[1,32,2048]{2,1,0:T(8,128)(2,1)S(1)}, bf16[1,32,2048]{2,1,0:T(8,128)(2,1)S(1)}, u32[]{:S(2)}, u32[]{:S(2)}) collective-permute-start(bf16[1,32,2048]{2,1,0:T(8,128)(2,1)S(1)} %slice_bitcast_fusion.22), channel_id=1, source_target_pairs={{0,2},{1,3},{2,0},{3,1},{4,6},{5,7},{6,4},{7,5},{8,10},{9,11},{10,... | collective-permute-start | bytes 393224 | tf_op jit(solution)/shard_map/ppermute | solution.py:18
  224.4 16.8 %collective-permute-start.33 = (bf16[1,32,2048]{2,1,0:T(8,128)(2,1)S(1)}, bf16[1,32,2048]{2,1,0:T(8,128)(2,1)S(1)}, u32[]{:S(2)}, u32[]{:S(2)}) collective-permute-start(bf16[1,32,2048]{2,1,0:T(8,128)(2,1)S(1)} %slice_bitcast_fusion.20), channel_id=1, source_target_pairs={{0,2},{1,3},{2,0},{3,1},{4,6},{5,7},{6,4},{7,5},{8,10},{9,11},{10,... | collective-permute-start | bytes 393224 | tf_op jit(solution)/shard_map/ppermute | solution.py:18
  229.8 8.2 %collective-permute-start.41 = (f32[2048]{0:T(1024)S(1)}, f32[2048]{0:T(1024)S(1)}, u32[]{:S(2)}, u32[]{:S(2)}) collective-permute-start(f32[2048]{0:T(1024)S(1)} %get-tuple-element.56), channel_id=1, source_target_pairs={{0,16},{16,0},{1,17},{17,1},{2,18},{18,2},{3,19},{19,3},{4,20},{20... | collective-permute-start | bytes 24584 | tf_op jit(solution)/shard_map/ppermute | solution.py:18
  237.3 8.4 %collective-permute-start.20 = (bf16[1,32,2048]{2,1,0:T(8,128)(2,1)S(1)}, bf16[1,32,2048]{2,1,0:T(8,128)(2,1)S(1)}, u32[]{:S(2)}, u32[]{:S(2)}) collective-permute-start(bf16[1,32,2048]{2,1,0:T(8,128)(2,1)S(1)} %bitcast.280), channel_id=1, source_target_pairs={{0,2},{1,3},{2,0},{3,1},{4,6},{5,7},{6,4},{7,5},{8,10},{9,11},{10,... | collective-permute-start | bytes 393224 | tf_op jit(solution)/shard_map/ppermute | solution.py:18
  238.0 5.1 %collective-permute-start.42 = (f32[2048]{0:T(1024)S(1)}, f32[2048]{0:T(1024)S(1)}, u32[]{:S(2)}, u32[]{:S(2)}) collective-permute-start(f32[2048]{0:T(1024)S(1)} %add.272), channel_id=1, source_target_pairs={{0,1},{1,0},{2,3},{3,2},{4,5},{5,4},{6,7},{7,6},{8,9},{9,8},{10,11... | collective-permute-start | bytes 24584 | tf_op jit(solution)/shard_map/ppermute | solution.py:18
  241.5 6.8 %collective-permute-start.37 = (bf16[1,32,2048]{2,1,0:T(8,128)(2,1)S(1)}, bf16[1,32,2048]{2,1,0:T(8,128)(2,1)S(1)}, u32[]{:S(2)}, u32[]{:S(2)}) collective-permute-start(bf16[1,32,2048]{2,1,0:T(8,128)(2,1)S(1)} %bitcast.282), channel_id=1, source_target_pairs={{0,2},{1,3},{2,0},{3,1},{4,6},{5,7},{6,4},{7,5},{8,10},{9,11},{10,... | collective-permute-start | bytes 393224 | tf_op jit(solution)/shard_map/ppermute | solution.py:18
  243.1 5.3 %collective-permute-start.43 = (f32[2048]{0:T(1024)S(1)}, f32[2048]{0:T(1024)S(1)}, u32[]{:S(2)}, u32[]{:S(2)}) collective-permute-start(f32[2048]{0:T(1024)S(1)} %add.273), channel_id=1, source_target_pairs={{0,2},{1,3},{2,0},{3,1},{4,6},{5,7},{6,4},{7,5},{8,10},{9,11},{10,... | collective-permute-start | bytes 24584 | tf_op jit(solution)/shard_map/ppermute | solution.py:18
  245.8 6.4 %collective-permute-start.21 = (bf16[2,32,2048]{2,1,0:T(8,128)(2,1)S(1)}, bf16[2,32,2048]{2,1,0:T(8,128)(2,1)S(1)}, u32[]{:S(2)}, u32[]{:S(2)}) collective-permute-start(bf16[2,32,2048]{2,1,0:T(8,128)(2,1)S(1)} %get-tuple-element.77), channel_id=1, source_target_pairs={{0,1},{1,0},{2,3},{3,2},{4,5},{5,4},{6,7},{7,6},{8,9},{9,8},{10,11... | collective-permute-start | bytes 786440 | tf_op jit(solution)/shard_map/ppermute | solution.py:18
  248.3 6.7 %collective-permute-start.38 = (bf16[2,32,2048]{2,1,0:T(8,128)(2,1)S(1)}, bf16[2,32,2048]{2,1,0:T(8,128)(2,1)S(1)}, u32[]{:S(2)}, u32[]{:S(2)}) collective-permute-start(bf16[2,32,2048]{2,1,0:T(8,128)(2,1)S(1)} %get-tuple-element.75), channel_id=1, source_target_pairs={{0,1},{1,0},{2,3},{3,2},{4,5},{5,4},{6,7},{7,6},{8,9},{9,8},{10,11... | collective-permute-start | bytes 786440 | tf_op jit(solution)/shard_map/ppermute | solution.py:18
  (60 other events, 571.6 us)
